TPU v7x, 32 devices: a whole 2x2x4 slice. The times are simulated.
32 devices in a mesh: tiles: 2 (over x), morton: 16 (over z, y, core).
Axes of the slice: x: 2, y: 2, z: 4, core: 2. Of those that a mesh axis runs over, the one named last changes fastest.
Arguments:
- features: bfloat16 [256, 512, 64], P(('tiles', 'morton')), parts along dimension 0, may hold values from -6 to 6
- neighbours: int32 [256, 27], P(('tiles', 'morton')), parts along dimension 0, may hold values from -1 to 127, as said below
- occupancy: int32 [256, 16], P(('tiles', 'morton')), parts along dimension 0, may hold values from -2147483648 to 2147483647, as said below
- conv_one: bfloat16 [27, 64, 64], replicated, may hold values from -0.21875 to 0.21875
- first_reduce_kernel: bfloat16 [8, 64, 128], replicated, may hold values from -0.5 to 0.5
- conv_two: bfloat16 [27, 128, 128], replicated, may hold values from -0.1875 to 0.1875
- second_reduce_kernel: bfloat16 [8, 128, 256], replicated, may hold values from -0.375 to 0.375
- conv_three: bfloat16 [27, 256, 256], replicated, may hold values from -0.125 to 0.125
Outputs:
- first_level_features: bfloat16 [256, 512, 64], P(('tiles', 'morton')), parts along dimension 0
- second_level_features: bfloat16 [256, 64, 128], P(('tiles', 'morton')), parts along dimension 0
- skip_three: bfloat16 [256, 8, 256], P(('tiles', 'morton')), parts along dimension 0
There are 2 independent parts, one for each index of `tiles`. A program takes and returns all parts, laid end to end along the dimension named above; an argument that names none is the same for every part. Nothing has to cross between parts.
Inputs may be any that keep to these rules, and one draw needn't show every extreme that they name: `neighbours`: bricks are numbered by x slice, then by cell of the slice's 4 x 4 cross-section in rising order, 8 occupied bricks to a slice. Entry 9 (a+1) + 3 (c+1) + (e+1) of a brick's row is the number of the brick at offset (a, c, e), or -1 if that cell is empty or outside the tile; entry 13 is the brick itself. Every neighbour lies in the brick's own slice or in an adjacent one. Bit k, the lowest being bit 0, of word w of a brick's row is the occupancy of voxel 32 w + k; bit 31 is the sign bit of the word.
All inputs are finite; a program needn't handle non-finite values.
Results may differ from a plain program's by a relative error of at most 0.008.
Values may be sent and summed in bfloat16 or wider, within the bound.
A program may use at most 128 MiB of HBM per device.

v0:
```python
import jax
import jax.numpy as jnp
from jax import lax
from jax.experimental import pallas as pl
from jax.experimental.pallas import tpu as pltpu
from jax.sharding import PartitionSpec as P

BRICKS = 8
LANES = 512
F32 = jnp.float32
BF16 = jnp.bfloat16


def iota(shape, dim):
    return lax.broadcasted_iota(jnp.int32, shape, dim)


def band_pairs(source, band):
    @pl.loop(0, 9)
    def _(tap):
        minus, same, plus = (source[3 * tap + e] for e in range(3))
        zero = jnp.zeros_like(same)
        low = jnp.concatenate([same, minus], axis=1)
        high = jnp.concatenate([plus, same], axis=1)
        before = jnp.concatenate([minus, zero], axis=1)
        after = jnp.concatenate([zero, plus], axis=1)
        blank = jnp.zeros((64, 128), BF16)
        rows = (
            (blank, blank), (before, blank),
            (low, blank), (high, before),
            (after, low), (blank, high),
            (blank, after), (blank, blank),
        )
        for at, (left, right) in enumerate(rows):
            band[tap, at * 64 : at * 64 + 64, 0:128] = left
            band[tap, at * 64 : at * 64 + 64, 128:256] = right


def band_single(source, band):
    @pl.loop(0, 9)
    def _(tap):
        minus, same, plus = (source[3 * tap + e] for e in range(3))
        blank = jnp.zeros_like(same)
        rows = ((minus, blank), (same, minus), (plus, same), (blank, plus))
        for at, (left, right) in enumerate(rows):
            band[tap, at * 128 : at * 128 + 128, 0:128] = left
            band[tap, at * 128 : at * 128 + 128, 128:256] = right


def assemble(side, halo, nb, sources, cols):
    row = iota((8, LANES + 2 * halo), 0)

    def source(brick, tap):
        number = nb[brick, tap]
        return jnp.where(number < 0, BRICKS, lax.rem(number, BRICKS))

    @pl.loop(0, BRICKS // 2)
    def _(pair):
        for dx, ref in sources:
            index = [
                [[source(2 * pair + b, 9 * dx + 3 * dy + dz) for dz in range(3)] for dy in range(3)]
                for b in range(2)
            ]
            for plane in range(side if dx == 1 else 1):
                at = slice(8 * plane, 8 * plane + 8)
                shifted = [[], [], []]
                for b in range(2):
                    views = []
                    for dy in range(3):
                        before, here, after = index[b][dy]
                        views.append(
                            jnp.concatenate(
                                [
                                    ref[before, at, LANES - halo : LANES],
                                    ref[here, at, :],
                                    ref[after, at, 0:halo],
                                ],
                                axis=1,
                            )
                        )
                    back, mid, front = views
                    shifted[0].append(
                        jnp.where(
                            row == 0,
                            pltpu.roll(back, (9 - side) % 8, 0),
                            pltpu.roll(mid, 1, 0),
                        )
                    )
                    shifted[1].append(mid)
                    shifted[2].append(
                        jnp.where(
                            row == side - 1,
                            pltpu.roll(front, side - 1, 0),
                            pltpu.roll(mid, 7, 0),
                        )
                    )
                to = plane + 1 if dx == 1 else (0 if dx == 0 else side + 1)
                rows = pl.ds(pl.multiple_of(16 * pair, 16), 16)
                for c in range(3):
                    cols[c, to, rows, :] = jnp.concatenate(shifted[c], axis=0).astype(BF16)


def convolve(side, depth, cols, weights, finish):
    chunk = min(side, 4)
    matrix = jnp.concatenate([weights(tap) for tap in range(9)], axis=0)
    for half in range(2):
        lanes = slice(256 * half, 256 * half + depth)
        for first in range(0, side, chunk):
            left = jnp.concatenate(
                [
                    cols[c, first + a : first + a + chunk, :, lanes].reshape(chunk * 64, depth)
                    for a in range(3)
                    for c in range(3)
                ],
                axis=1,
            )
            sums = jnp.dot(left, matrix, preferred_element_type=F32)
            finish(half, first, sums.reshape(chunk, BRICKS, 8, 256))


def rounded(value):
    return value.astype(BF16).astype(F32)


def pool_bits(bits, fine_side, temp, pooled):
    half = fine_side // 2
    count = BRICKS * half * 8
    joined = bits[0 : BRICKS * fine_side * 8, :].reshape(BRICKS * half, 2, 8, 128)
    temp[0:count, :] = (joined[:, 0] | joined[:, 1]).reshape(count, 128)
    temp[count : count + 16, :] = jnp.zeros((16, 128), jnp.int32)
    for at in range(BRICKS * half):
        even = temp[pl.ds(8 * at, 8, stride=2), :]
        odd = temp[pl.ds(8 * at + 1, 8, stride=2), :]
        pooled[8 * at : 8 * at + 8, :] = even | odd


def reduce_level(side, block, fine, kernel, bits, bit_width, emit):
    half = side // 2
    width = 2 * block
    for at in range(LANES // width):
        parts = []
        for ci in range(2):
            for cj in range(2):
                pieces = []
                for lane in range(at * width, (at + 1) * width, 128):
                    pieces.append(
                        jnp.concatenate(
                            [
                                fine[lane // 128, pl.ds((b * side + 2 * i + ci) * 8 + cj, 8, stride=2), :]
                                for b in range(BRICKS)
                                for i in range(half)
                            ],
                            axis=0,
                        )
                    )
                parts += pieces
        left = jnp.concatenate(parts, axis=1).astype(BF16)
        sums = jnp.dot(left, kernel, preferred_element_type=F32)
        mask = ((bits[0 : BRICKS * half * 8, :] >> (bit_width * at)) & ((1 << bit_width) - 1)) != 0
        wide = sums.shape[1]
        for lane in range(0, wide, 128):
            emit(
                at * wide + lane,
                jnp.where(mask, jnp.maximum(sums[:, lane : lane + 128], 0.0), 0.0),
            )


def relayout(temp, lane):
    for q in range(4):
        even = temp[pl.ds(2 * q, 64, stride=8), :]
        odd = temp[pl.ds(2 * q + 1, 64, stride=8), :]
        yield q, jnp.where(lane < 64, even, pltpu.roll(odd, 64, 1))


def fused(nb, feat, occ, conv_one, kernel_one, conv_two_hbm, kernel_two_hbm, conv_three_hbm,
          out_one, out_two, cols_three, bits_three, conv_three,
          own_one, own_two, own_three, low, high, cols_one, cols_two,
          band_one, band_two, conv_two, kernel_two,
          fine, temp, wide, bits_one, bits_two, bits_temp,
          outgoing, incoming, load_sems, send_sems, recv_sems):
    me = lax.axis_index("morton")
    count = lax.axis_size("morton")
    has_low, has_high = me > 0, me < count - 1
    sides = ((has_low, me - 1), (has_high, me + 1))

    loads = [
        pltpu.make_async_copy(source, target, load_sems.at[at])
        for at, (source, target) in enumerate(
            ((conv_two_hbm, conv_two), (kernel_two_hbm, kernel_two), (conv_three_hbm, conv_three))
        )
    ]
    for load in loads:
        load.start()

    barrier = pltpu.get_barrier_semaphore()
    for there, device in sides:
        @pl.when(there)
        def _():
            pl.semaphore_signal(barrier, inc=1, device_id={"morton": device},
                                device_id_type=pl.DeviceIdType.MESH)

    def transfer(level, to):
        return pltpu.make_async_remote_copy(
            src_ref=outgoing.at[level, to],
            dst_ref=incoming.at[level, 1 - to],
            send_sem=send_sems.at[level, to],
            recv_sem=recv_sems.at[level, 1 - to],
            device_id={"morton": sides[to][1]},
            device_id_type=pl.DeviceIdType.MESH,
        )

    def send(level):
        for to in range(2):
            @pl.when(sides[to][0])
            def _():
                transfer(level, to).start()

    def receive(level):
        for source in range(2):
            @pl.when(sides[source][0])
            def _():
                transfer(level, 1 - source).wait_recv()
                (low, high)[source][0:BRICKS] = incoming[level, source].astype(F32)

    lane = iota((64, 128), 1)
    row = iota((64, 16), 0)
    column = iota((64, 16), 1)
    upper = (lane >= 64).astype(jnp.int32)
    for ref in (own_one, own_two, own_three):
        ref[BRICKS] = jnp.zeros(ref.shape[1:], F32)
    for ref in (low, high):
        ref[...] = jnp.zeros(ref.shape, F32)

    @pl.loop(0, BRICKS)
    def _(b):
        words = jnp.broadcast_to(occ[pl.ds(b, 1), :], (64, 16))
        octet = (words >> (8 * (row % 4))) & 255
        picked = jnp.where(column == row // 4, octet.astype(F32), 0.0)
        mask = jnp.broadcast_to(jnp.sum(picked, axis=1, keepdims=True), (64, 128)).astype(jnp.int32)
        bits_one[pl.ds(pl.multiple_of(64 * b, 64), 64), :] = mask
        temp[:, 0:64] = feat[b].astype(F32).T
        for q, both in relayout(temp, lane):
            value = jnp.where(((mask >> (2 * q + upper)) & 1) != 0, both, 0.0)
            lanes = slice(128 * q, 128 * q + 128)
            own_one[b, :, lanes] = value
            outgoing[0, 0, b, :, lanes] = value[0:8].astype(BF16)
            outgoing[0, 1, b, :, lanes] = value[56:64].astype(BF16)

    pl.semaphore_wait(barrier, jnp.minimum(me, 1) + jnp.minimum(count - 1 - me, 1))
    send(0)
    band_pairs(conv_one, band_one)
    assemble(8, 128, nb, ((1, own_one),), cols_one)
    loads[0].wait()
    band_single(conv_two, band_two)
    receive(0)
    assemble(8, 128, nb, ((0, low), (2, high)), cols_one)

    small_upper = (iota((8, 128), 1) >= 64).astype(jnp.int32)

    def finish_one(half, first, sums):
        for p in range(sums.shape[0]):
            for b in range(BRICKS):
                at = b * 64 + (first + p) * 8
                mask = bits_one[at : at + 8, :]
                for part in range(2):
                    q = 2 * half + part
                    fine[q, at : at + 8, :] = rounded(
                        jnp.where(
                            ((mask >> (2 * q + small_upper)) & 1) != 0,
                            jnp.maximum(sums[p, b, :, 128 * part : 128 * part + 128], 0.0),
                            0.0,
                        )
                    )

    convolve(8, 512, cols_one, lambda tap: band_one[tap], finish_one)
    fine[:, 512:528, :] = jnp.zeros((4, 16, 128), F32)
    pool_bits(bits_one, 8, bits_temp, bits_two)

    def emit_into(own, level, planes):
        def emit(lane_at, value):
            value = rounded(value).reshape(BRICKS, 8 * planes, 128)
            lanes = slice(lane_at, lane_at + 128)
            own[0:BRICKS, :, lanes] = value
            outgoing[level, 0, :, :, lanes] = value[:, 0:8].astype(BF16)
            outgoing[level, 1, :, :, lanes] = value[:, 8 * planes - 8 :].astype(BF16)
        return emit

    reduce_level(8, 64, fine, kernel_one[...], bits_two, 2, emit_into(own_two, 1, 4))
    send(1)
    assemble(4, 128, nb, ((1, own_two),), cols_two)

    @pl.loop(0, BRICKS)
    def _(b):
        for q in range(4):
            both = fine[q, pl.ds(pl.multiple_of(64 * b, 64), 64), :]
            wide[pl.ds(2 * q, 64, stride=8), :] = both
            wide[pl.ds(2 * q + 1, 64, stride=8), :] = pltpu.roll(both, 64, 1)
        out_one[b] = wide[:, 0:64].T.astype(BF16)

    receive(1)
    assemble(4, 128, nb, ((0, low), (2, high)), cols_two)

    def finish_two(half, first, sums):
        for p in range(sums.shape[0]):
            for b in range(BRICKS):
                at = b * 32 + (first + p) * 8
                mask = bits_two[at : at + 8, :]
                for part in range(2):
                    q = 2 * half + part
                    fine[q, at : at + 8, :] = rounded(
                        jnp.where(
                            ((mask >> (2 * q)) & 3) != 0,
                            jnp.maximum(sums[p, b, :, 128 * part : 128 * part + 128], 0.0),
                            0.0,
                        )
                    )

    convolve(4, 512, cols_two, lambda tap: band_two[tap], finish_two)
    pool_bits(bits_two, 4, bits_temp, bits_three)
    loads[1].wait()
    reduce_level(4, 128, fine, kernel_two[...], bits_three, 4, emit_into(own_three, 2, 2))
    send(2)
    assemble(2, 256, nb, ((1, own_three),), cols_three)
    for b in range(BRICKS):
        for i in range(4):
            for k in range(4):
                at = b * 32 + 8 * i
                wide[pl.ds(64 * b + 16 * i + k, 4, stride=4), :] = fine[k, at : at + 4, :]
    out_two[...] = wide[...].reshape(BRICKS, 64, 128).astype(BF16)
    receive(2)
    assemble(2, 256, nb, ((0, low), (2, high)), cols_three)

    loads[2].wait()
    for level in range(3):
        for to in range(2):
            @pl.when(sides[to][0])
            def _():
                transfer(level, to).wait_send()


def last_level(one, two, cols_three, bits_three, conv_three,
               out_one, out_two, out_three, wide_three):
    out_one[...] = one[...]
    out_two[...] = two[...]

    def finish_three(half, first, sums):
        for p in range(sums.shape[0]):
            for b in range(BRICKS):
                at = b * 16 + (first + p) * 8
                mask = ((bits_three[at : at + 8, :] >> (4 * half)) & 15) != 0
                for part in range(2):
                    value = jnp.where(
                        mask, jnp.maximum(sums[p, b, :, 128 * part : 128 * part + 128], 0.0), 0.0
                    )
                    wide_three[part, pl.ds(8 * b + 4 * (first + p) + half, 2, stride=2), :] = value[0:2]

    convolve(2, 768, cols_three, lambda tap: conv_three[3 * tap : 3 * tap + 3].reshape(768, 256), finish_three)
    for part in range(2):
        out_three[:, :, 128 * part : 128 * part + 128] = (
            wide_three[part].reshape(BRICKS, 8, 128).astype(BF16)
        )


def on_device(features, neighbours, occupancy, conv_one, first_reduce_kernel,
              conv_two, second_reduce_kernel, conv_three):
    vm = pl.BlockSpec(memory_space=pltpu.VMEM)
    hbm = pl.BlockSpec(memory_space=pltpu.HBM)
    kernel_two = second_reduce_kernel.reshape(1024, 256)
    scratch = [
        ((BRICKS + 1, 64, LANES), F32), ((BRICKS + 1, 32, LANES), F32),
        ((BRICKS + 1, 16, LANES), F32), ((BRICKS + 1, 8, LANES), F32),
        ((BRICKS + 1, 8, LANES), F32),
        ((3, 10, 64, 768), BF16), ((3, 6, 64, 768), BF16),
        ((9, 512, 256), BF16), ((9, 512, 256), BF16),
        (conv_two.shape, BF16), (kernel_two.shape, BF16),
        ((4, 528, 128), F32), ((512, 128), F32), ((512, 128), F32),
        ((512, 128), jnp.int32), ((256, 128), jnp.int32),
        ((272, 128), jnp.int32),
        ((3, 2, BRICKS, 8, LANES), BF16), ((3, 2, BRICKS, 8, LANES), BF16),
    ]
    shapes = [
        jax.ShapeDtypeStruct((BRICKS, 64, 512), BF16),
        jax.ShapeDtypeStruct((BRICKS, 64, 128), BF16),
    ]
    first, second, cols, bits, weights = pl.pallas_call(
        fused,
        out_shape=shapes
        + [
            jax.ShapeDtypeStruct((3, 4, 64, 1024), BF16),
            jax.ShapeDtypeStruct((128, 128), jnp.int32),
            jax.ShapeDtypeStruct(conv_three.shape, BF16),
        ],
        in_specs=[pl.BlockSpec(memory_space=pltpu.SMEM), vm, vm, vm, vm, hbm, hbm, hbm],
        out_specs=[vm] * 5,
        scratch_shapes=[pltpu.VMEM(shape, dtype) for shape, dtype in scratch]
        + [pltpu.SemaphoreType.DMA((3,)), pltpu.SemaphoreType.DMA((3, 2)),
           pltpu.SemaphoreType.DMA((3, 2))],
        compiler_params=pltpu.CompilerParams(
            collective_id=0, has_side_effects=True, vmem_limit_bytes=36 << 20
        ),
    )(*(
        pltpu.with_memory_space_constraint(x, pltpu.HBM)
        for x in (neighbours, jnp.swapaxes(features, 1, 2), occupancy, conv_one,
                  first_reduce_kernel.reshape(512, 128), conv_two, kernel_two, conv_three)
    ))
    first, second, third = pl.pallas_call(
        last_level,
        out_shape=shapes + [jax.ShapeDtypeStruct((BRICKS, 8, 256), BF16)],
        in_specs=[vm] * 5,
        out_specs=[vm] * 3,
        scratch_shapes=[pltpu.VMEM((2, 64, 128), F32)],
        compiler_params=pltpu.CompilerParams(vmem_limit_bytes=16 << 20),
    )(first, second, cols, bits, weights)
    return jnp.swapaxes(first, 1, 2), second, third


def solution(mesh):
    split = P(("tiles", "morton"), None, None)
    flat = P(("tiles", "morton"), None)
    return jax.shard_map(
        on_device,
        mesh=mesh,
        in_specs=(split, flat, flat, P(), P(), P(), P(), P()),
        out_specs=(split, split, split),
        check_vma=False,
    )
```

profile of v0, /device:TPU:7, one launch (start us, length us, event | category | flops | bytes accessed | tf_op | source)
XLA Modules:
  0.0 22.0 jit_solution(9352615177896249546)
XLA Ops:
  0.6 19.6 %shard_map.103 = (bf16[8,64,512]{2,1,0:T(8,128)(2,1)S(1)}, bf16[8,64,128]{2,1,0:T(8,128)(2,1)S(1)}, bf16[3,4,64,1024]{3,2,1,0:T(8,128)(2,1)S(1)}, s32[128,128]{1,0:T(8,128)S(1)}, bf16[27,256,256]{2,1,0:T(8,128)(2,1)S(1)}) custom-call(s32[8,27]{1,0:T(8,128)} %nb.1, bf16[8,64,512]{2,1,0:T(8,128)(2,1)} %bitcast.4, s32[8,16]{1,0:T(8,128)} %occ.1, ...), custom_call_target="tpu_custom_call" | custom-call | tf_op jit(solution)/shard_map/pallas_call | solution.py:385
  20.2 1.8 %shard_map.104 = (bf16[8,64,512]{2,1,0:T(8,128)(2,1)}, bf16[8,64,128]{2,1,0:T(8,128)(2,1)}, bf16[8,8,256]{2,1,0:T(8,128)(2,1)}) custom-call(bf16[8,64,512]{2,1,0:T(8,128)(2,1)S(1)} %get-tuple-element.11.one, bf16[8,64,128]{2,1,0:T(8,128)(2,1)S(1)} %get-tuple-element.12.two, bf16[3,4,64,1024]{3,2,1,0:T(8,128)(2,1)S(1)} %get-tuple-element.13.cols_three, ...), custom_call_target="tpu_custom_call" | custom-call | tf_op jit(solution)/shard_map/pallas_call | solution.py:406
where the time goes:
time: 22.2 us; the launch traced here: 22 us
  Pallas kernels  21.4 us (96%)
  between operations  0.64 us (3%)
    pallas_call x1, Pallas kernels, on_device(): pl.pallas_call(fused, out_shape=shapes + [jax.ShapeDtypeStruct((3, 4, 64,...  19.6 us
    pallas_call x1, Pallas kernels, on_device(): pl.pallas_call(last_level, out_shape=shapes + [jax.ShapeDtypeStruct((BRIC...  1.82 us

commit v1 on v0

v1 whole, which is shorter than its diff:
```python
import jax
import jax.numpy as jnp
from jax import lax
from jax.experimental import pallas as pl
from jax.experimental.pallas import tpu as pltpu
from jax.sharding import PartitionSpec as P

BRICKS = 8
F32 = jnp.float32
BF16 = jnp.bfloat16
I32 = jnp.int32


def iota(shape, dim):
    return lax.broadcasted_iota(I32, shape, dim)


def pack(lower, upper):
    return jnp.concatenate([lower, upper], axis=0).astype(BF16)


def halves(tile):
    wide = tile.astype(F32)
    return wide[0:8], wide[8:16]


def windows_one(own, before, after):
    low_lanes = iota((BRICKS, 128), 1) < 64
    return (
        (own[0], own[2]),
        (own[1], own[3]),
        (jnp.where(low_lanes, own[2], before(3)), jnp.where(low_lanes, after(0), own[1])),
    )


def windows_two(own, before, after):
    return ((own[0], own[2]), (own[1], own[3]), (own[2], after(0)), (before(3), own[1]))


def windows_three(own, before, after):
    return (
        (before(2), own[0]), (before(3), own[1]),
        (own[0], own[2]), (own[1], own[3]),
        (own[2], after(0)), (own[3], after(1)),
    )


def fill(put, tiles, dx, dy, near, windows):
    first = 9 * dx + 3 * dy

    def moved(q, tap):
        number = near[tap]
        picked = jnp.take_along_axis(tiles[q], number & (BRICKS - 1), axis=0, mode="promise_in_bounds")
        return jnp.where(number >= 0, picked, 0.0)

    own = tiles if first == 12 else [moved(q, first + 1) for q in range(4)]
    for at, (lower, upper) in enumerate(
        windows(own, lambda q: moved(q, first), lambda q: moved(q, first + 2))
    ):
        put(at, pack(lower, upper))


def fill_plane(side, cols, to, source, dx, near, windows):
    for j in range(side):
        tiles = source(j)
        places = [(1, j + 1)] + [(0, 0)] * (j == side - 1) + [(2, side + 1)] * (j == 0)
        for dy, column in places:
            def put(at, value, column=column):
                cols[to, column, :, 128 * at : 128 * at + 128] = value
            fill(put, tiles, dx, dy, near, windows)


def convolve(side, planes, cols, band):
    width = cols.shape[-1]
    left = jnp.concatenate(
        [
            jnp.concatenate(
                [cols[plane + a, c : c + side].reshape(side * 16, width) for plane in planes], axis=0
            )
            for a in range(3)
            for c in range(3)
        ],
        axis=1,
    )
    return jnp.dot(left, band, preferred_element_type=F32)


def build_band_one(source, band):
    @pl.loop(0, 9)
    def _(pair):
        minus, same, plus = (source[3 * pair + e] for e in range(3))
        zero = jnp.zeros_like(same)
        blank = jnp.zeros((64, 128), BF16)
        low = jnp.concatenate([same, minus], axis=1)
        high = jnp.concatenate([plus, same], axis=1)
        before = jnp.concatenate([minus, zero], axis=1)
        after = jnp.concatenate([zero, plus], axis=1)
        rows = ((low, blank), (high, before), (after, low), (blank, high), (blank, after), (before, blank))
        for at, (left, right) in enumerate(rows):
            to = pl.ds(pl.multiple_of(384 * pair + 64 * at, 64), 64)
            band[to, 0:128] = left
            band[to, 128:256] = right


def build_band_two(source, band):
    @pl.loop(0, 9)
    def _(pair):
        minus, same, plus = (source[3 * pair + e] for e in range(3))
        blank = jnp.zeros_like(same)
        rows = ((same, minus), (plus, same), (blank, plus), (minus, blank))
        for at, (left, right) in enumerate(rows):
            to = pl.ds(pl.multiple_of(512 * pair + 128 * at, 128), 128)
            band[to, 0:128] = left
            band[to, 128:256] = right


def fused(nb, feat, occ, conv_one, kernel_one, conv_two_hbm, kernel_two_hbm, conv_three_hbm,
          out_one, out_two, cols_three, pooled_three, conv_three,
          field_one, field_two, field_three, cols_one, cols_two, done_one, done_two,
          band_one, band_two, conv_two, kernel_two, near, words, tests, pooled_two, wide,
          outgoing, incoming, load_sems, send_sems, recv_sems):
    me = lax.axis_index("morton")
    count = lax.axis_size("morton")
    has_low, has_high = me > 0, me < count - 1
    sides = ((has_low, me - 1), (has_high, me + 1))
    extents = (8, 4, 2)

    loads = [
        pltpu.make_async_copy(source, target, load_sems.at[at])
        for at, (source, target) in enumerate(
            ((conv_two_hbm, conv_two), (kernel_two_hbm, kernel_two), (conv_three_hbm, conv_three))
        )
    ]
    for load in loads:
        load.start()

    barrier = pltpu.get_barrier_semaphore()
    for there, device in sides:
        @pl.when(there)
        def _():
            pl.semaphore_signal(barrier, inc=1, device_id={"morton": device},
                                device_id_type=pl.DeviceIdType.MESH)

    def transfer(level, to):
        return pltpu.make_async_remote_copy(
            src_ref=outgoing.at[level, to, 0 : extents[level]],
            dst_ref=incoming.at[level, 1 - to, 0 : extents[level]],
            send_sem=send_sems.at[level, to],
            recv_sem=recv_sems.at[level, 1 - to],
            device_id={"morton": sides[to][1]},
            device_id_type=pl.DeviceIdType.MESH,
        )

    def send(level):
        for to in range(2):
            @pl.when(sides[to][0])
            def _():
                transfer(level, to).start()

    def receive(level, cols, windows):
        side = extents[level]
        for source in range(2):
            @pl.when(sides[source][0])
            def _():
                transfer(level, 1 - source).wait_recv()

            def arrived(j, source=source):
                pieces = [halves(incoming[level, source, j, :, 128 * t : 128 * t + 128]) for t in range(2)]
                return [pieces[q % 2][q // 2] for q in range(4)]

            fill_plane(side, cols, (0, side + 1)[source], arrived, 2 * source, near, windows)

    def stage(level, to, j, tiles):
        for t in range(2):
            outgoing[level, to, j, :, 128 * t : 128 * t + 128] = pack(tiles[t], tiles[2 + t])

    for source in range(2):
        @pl.when(jnp.logical_not(sides[source][0]))
        def _():
            for level in range(3):
                incoming[level, source] = jnp.zeros(incoming.shape[2:], BF16)

    for tap in range(27):
        near[tap] = jnp.broadcast_to(nb[:, tap : tap + 1], (BRICKS, 128))
    for word in range(16):
        words[word] = jnp.broadcast_to(occ[:, word : word + 1], (BRICKS, 128))
    upper = (iota((BRICKS, 128), 1) >= 64).astype(I32)
    for at in range(16):
        tests[at] = jnp.left_shift(jnp.ones((BRICKS, 128), I32), 2 * at + upper)
    for i in range(4):
        for part in range(2):
            word = words[4 * i + part] | words[4 * i + 2 + part]
            for far in range(2):
                pooled_two[i, 2 * part + far] = (word >> (16 * far)) | (word >> (16 * far + 8))
    for i in range(2):
        for j in range(2):
            pooled_three[i, j] = (
                pooled_two[2 * i, 2 * j] | pooled_two[2 * i, 2 * j + 1]
                | pooled_two[2 * i + 1, 2 * j] | pooled_two[2 * i + 1, 2 * j + 1]
            )

    def keep_one(i, j, q, value):
        bit = words[2 * i + j // 4] & tests[4 * (j % 4) + q]
        return jnp.where(bit != 0, value, 0.0)

    choose = (iota((128, 256), 1) // 2 == iota((128, 256), 0)).astype(F32).astype(BF16)
    odd = iota((64, 256), 1) % 2 == 1
    for half in range(2):
        lanes = slice(256 * half, 256 * half + 256)
        for b in range(0, BRICKS, 2):
            rows = []
            for brick in (b, b + 1):
                value = feat[brick, :, lanes]
                zero = jnp.zeros_like(value)
                rows += [jnp.where(odd, zero, value), jnp.where(odd, value, zero)]
            both = lax.dot_general(
                choose, jnp.concatenate(rows, axis=0), (((1,), (1,)), ((), ())),
                preferred_element_type=F32,
            )
            for step in range(2):
                field_one[pl.ds(1024 * half + b + step, 128, stride=8), :] = (
                    both[:, 128 * step : 128 * step + 128]
                )

    def tile_at(i, j, q):
        return pl.ds(pl.multiple_of(256 * i + 32 * j + 8 * q, 8), 8)

    def own_one(i):
        def source(j):
            return [keep_one(i, j, q, field_one[tile_at(i, j, q), :]) for q in range(4)]
        return source

    for to, i in enumerate((0, 7)):
        def edge(j, to=to, i=i):
            tiles = own_one(i)(j)
            stage(0, to, j, tiles)
            return tiles
        fill_plane(8, cols_one, i + 1, edge, 1, near, windows_one)

    pl.semaphore_wait(barrier, jnp.minimum(me, 1) + jnp.minimum(count - 1 - me, 1))
    send(0)
    build_band_one(conv_one, band_one)

    @pl.loop(1, 7)
    def _(i):
        fill_plane(8, cols_one, i + 1, own_one(i), 1, near, windows_one)

    loads[0].wait()
    build_band_two(conv_two, band_two)
    receive(0, cols_one, windows_one)

    def first_level(planes):
        sums = convolve(8, planes, cols_one, band_one[...])
        for p, i in enumerate(planes):
            for j in range(8):
                at = 128 * p + 16 * j
                for t in range(2):
                    lanes = slice(128 * t, 128 * t + 128)
                    tiles = []
                    for h in range(2):
                        q = 2 * h + t
                        value = keep_one(i, j, q, jnp.maximum(sums[at + 8 * h : at + 8 * h + 8, lanes], 0.0))
                        field_one[tile_at(i, j, q), :] = value
                        tiles.append(value)
                    done_one[i, j, :, lanes] = pack(*tiles)
        pooled = [planes[0] // 2, planes[2] // 2]
        left = jnp.concatenate(
            [
                jnp.concatenate(
                    [
                        done_one[2 * i + ci, 2 * j + cj, :, 128 * t : 128 * t + 128]
                        for t in range(2)
                        for i in pooled
                        for j in range(4)
                    ],
                    axis=0,
                )
                for ci in range(2)
                for cj in range(2)
            ],
            axis=1,
        )
        sums = jnp.dot(left, kernel_one[...], preferred_element_type=F32)
        for p, i in enumerate(pooled):
            for j in range(4):
                for t in range(2):
                    for h in range(2):
                        at = 128 * t + 64 * p + 16 * j + 8 * h
                        q = 2 * h + t
                        keep = (pooled_two[i, j] & (3 << (2 * q))) != 0
                        field_two[i, j, q] = jnp.where(keep, jnp.maximum(sums[at : at + 8], 0.0), 0.0)

    first_level((0, 1, 6, 7))
    for to, i in enumerate((0, 3)):
        for j in range(4):
            stage(1, to, j, [field_two[i, j, q] for q in range(4)])
    send(1)
    first_level((2, 3, 4, 5))

    for i in range(4):
        fill_plane(4, cols_two, i + 1, lambda j, i=i: [field_two[i, j, q] for q in range(4)],
                   1, near, windows_two)
    receive(1, cols_two, windows_two)

    sums = convolve(4, range(4), cols_two, band_two[...])
    for i in range(4):
        for j in range(4):
            at = 64 * i + 16 * j
            for t in range(2):
                lanes = slice(128 * t, 128 * t + 128)
                tiles = []
                for h in range(2):
                    q = 2 * h + t
                    keep = (pooled_two[i, j] & (3 << (2 * q))) != 0
                    value = jnp.where(keep, jnp.maximum(sums[at + 8 * h : at + 8 * h + 8, lanes], 0.0), 0.0)
                    wide[pl.ds(16 * i + 4 * j + q, 8, stride=64), :] = value
                    tiles.append(value)
                done_two[i, j, :, lanes] = pack(*tiles)
    loads[1].wait()
    left = jnp.concatenate(
        [
            jnp.concatenate(
                [done_two[2 * i + ci, 2 * j + cj] for i in range(2) for j in range(2)], axis=0
            )
            for ci in range(2)
            for cj in range(2)
        ],
        axis=1,
    )
    sums = jnp.dot(left, kernel_two[...], preferred_element_type=F32)
    for i in range(2):
        for j in range(2):
            at = 32 * i + 16 * j
            for h in range(2):
                keep = (pooled_three[i, j] & (15 << (4 * h))) != 0
                for t in range(2):
                    value = sums[at + 8 * h : at + 8 * h + 8, 128 * t : 128 * t + 128]
                    field_three[i, j, 2 * h + t] = jnp.where(keep, jnp.maximum(value, 0.0), 0.0)
    for to in range(2):
        for j in range(2):
            stage(2, to, j, [field_three[to, j, q] for q in range(4)])
    send(2)

    for i in range(2):
        fill_plane(2, cols_three, i + 1, lambda j, i=i: [field_three[i, j, q] for q in range(4)],
                   1, near, windows_three)
    out_two[...] = wide[...].reshape(BRICKS, 64, 128).astype(BF16)

    spread = (
        iota((256, 256), 1) == 2 * (iota((256, 256), 0) % 128) + iota((256, 256), 0) // 128
    ).astype(F32).astype(BF16)
    for half in range(2):
        left = []
        for b in range(BRICKS):
            turned = field_one[pl.ds(1024 * half + b, 128, stride=8), :].T
            left.append(jnp.concatenate([turned[0:64], turned[64:128]], axis=1).astype(BF16))
        sums = jnp.dot(jnp.concatenate(left, axis=0), spread, preferred_element_type=F32)
        for b in range(BRICKS):
            out_one[b, :, 256 * half : 256 * half + 256] = sums[64 * b : 64 * b + 64].astype(BF16)

    receive(2, cols_three, windows_three)

    loads[2].wait()
    for level in range(3):
        for to in range(2):
            @pl.when(sides[to][0])
            def _():
                transfer(level, to).wait_send()


def last_level(one, two, cols_three, pooled_three, conv_three,
               out_one, out_two, out_three, wide, sems):
    copies = [
        pltpu.make_async_copy(one, out_one, sems.at[0]),
        pltpu.make_async_copy(two, out_two, sems.at[1]),
    ]
    for copy in copies:
        copy.start()
    sums = convolve(2, range(2), cols_three, conv_three[...].reshape(27 * 256, 256))
    for i in range(2):
        for j in range(2):
            at = 32 * i + 16 * j
            for h in range(2):
                keep = (pooled_three[i, j] & (15 << (4 * h))) != 0
                for t in range(2):
                    value = sums[at + 8 * h : at + 8 * h + 8, 128 * t : 128 * t + 128]
                    wide[t, pl.ds(4 * i + 2 * j + h, 8, stride=8), :] = jnp.where(
                        keep, jnp.maximum(value, 0.0), 0.0
                    )
    for t in range(2):
        out_three[:, :, 128 * t : 128 * t + 128] = wide[t].reshape(BRICKS, 8, 128).astype(BF16)
    for copy in copies:
        copy.wait()


def on_device(features, neighbours, occupancy, conv_one, first_reduce_kernel,
              conv_two, second_reduce_kernel, conv_three):
    vm = pl.BlockSpec(memory_space=pltpu.VMEM)
    hbm = pl.BlockSpec(memory_space=pltpu.HBM)
    kernel_two = second_reduce_kernel.reshape(1024, 256)
    scratch = [
        ((2048, 128), F32), ((4, 4, 4, BRICKS, 128), F32), ((2, 2, 4, BRICKS, 128), F32),
        ((10, 10, 16, 384), BF16), ((6, 6, 16, 512), BF16),
        ((8, 8, 16, 256), BF16), ((4, 4, 16, 256), BF16),
        ((9 * 384, 256), BF16), ((9 * 512, 256), BF16),
        (conv_two.shape, BF16), (kernel_two.shape, BF16),
        ((27, BRICKS, 128), I32), ((16, BRICKS, 128), I32), ((16, BRICKS, 128), I32),
        ((4, 4, BRICKS, 128), I32), ((512, 128), F32),
        ((3, 2, 8, 16, 256), BF16), ((3, 2, 8, 16, 256), BF16),
    ]
    shapes = [
        jax.ShapeDtypeStruct((BRICKS, 64, 512), BF16),
        jax.ShapeDtypeStruct((BRICKS, 64, 128), BF16),
    ]
    first, second, cols, pooled, weights = pl.pallas_call(
        fused,
        out_shape=shapes
        + [
            jax.ShapeDtypeStruct((4, 4, 16, 768), BF16),
            jax.ShapeDtypeStruct((2, 2, BRICKS, 128), I32),
            jax.ShapeDtypeStruct(conv_three.shape, BF16),
        ],
        in_specs=[vm, vm, vm, vm, vm, hbm, hbm, hbm],
        out_specs=[vm] * 5,
        scratch_shapes=[pltpu.VMEM(shape, dtype) for shape, dtype in scratch]
        + [pltpu.SemaphoreType.DMA((3,)), pltpu.SemaphoreType.DMA((3, 2)),
           pltpu.SemaphoreType.DMA((3, 2))],
        compiler_params=pltpu.CompilerParams(
            collective_id=0, has_side_effects=True, vmem_limit_bytes=36 << 20
        ),
    )(*(
        pltpu.with_memory_space_constraint(x, pltpu.HBM)
        for x in (neighbours, jnp.swapaxes(features, 1, 2), occupancy, conv_one,
                  first_reduce_kernel.reshape(512, 128), conv_two, kernel_two, conv_three)
    ))
    first, second, third = pl.pallas_call(
        last_level,
        out_shape=shapes + [jax.ShapeDtypeStruct((BRICKS, 8, 256), BF16)],
        in_specs=[vm] * 5,
        out_specs=[hbm, hbm, vm],
        scratch_shapes=[pltpu.VMEM((2, 64, 128), F32), pltpu.SemaphoreType.DMA((2,))],
        compiler_params=pltpu.CompilerParams(vmem_limit_bytes=16 << 20),
    )(first, second, cols, pooled, weights)
    return jnp.swapaxes(first, 1, 2), second, third


def solution(mesh):
    split = P(("tiles", "morton"), None, None)
    flat = P(("tiles", "morton"), None)
    return jax.shard_map(
        on_device,
        mesh=mesh,
        in_specs=(split, flat, flat, P(), P(), P(), P(), P()),
        out_specs=(split, split, split),
        check_vma=False,
    )
```

time: 22.2 us -> 18.1 us (0.82)
  Pallas kernels: 21.4 us -> 17.2 us
    pallas_call x1, Pallas kernels: 19.6 us -> 15.3 us  [on_device(): pl.pallas_call(fused, out_shape=shapes + [jax.ShapeDtypeStruct((4, 4, 16,...]
where the time goes in v1:
time: 18.1 us; the launch traced here: 17.9 us
  Pallas kernels  17.2 us (95%)
  between operations  0.64 us (4%)
    pallas_call x1, Pallas kernels, on_device(): pl.pallas_call(fused, out_shape=shapes + [jax.ShapeDtypeStruct((4, 4, 16,...  15.3 us
    pallas_call x1, Pallas kernels, on_device(): pl.pallas_call(last_level, out_shape=shapes + [jax.ShapeDtypeStruct((BRIC...  1.91 us

profile of v1, /device:TPU:7, one launch (start us, length us, event | category | flops | bytes accessed | tf_op | source)
XLA Modules:
  0.0 17.9 jit_solution(10832099583375101185)
XLA Ops:
  0.6 15.3 %shard_map.103 = (bf16[8,64,512]{2,1,0:T(8,128)(2,1)S(1)}, bf16[8,64,128]{2,1,0:T(8,128)(2,1)S(1)}, bf16[4,4,16,768]{3,2,1,0:T(8,128)(2,1)S(1)}, s32[2,2,8,128]{3,2,1,0:T(8,128)S(1)}, bf16[27,256,256]{2,1,0:T(8,128)(2,1)S(1)}) custom-call(s32[8,27]{1,0:T(8,128)} %nb.1, bf16[8,64,512]{2,1,0:T(8,128)(2,1)} %bitcast.4, s32[8,16]{1,0:T(8,128)} %occ.1, ...), custom_call_target="tpu_custom_call" | custom-call | tf_op jit(solution)/shard_map/pallas_call | solution.py:415
  16.0 1.9 %shard_map.104 = (bf16[8,64,512]{2,1,0:T(8,128)(2,1)}, bf16[8,64,128]{2,1,0:T(8,128)(2,1)}, bf16[8,8,256]{2,1,0:T(8,128)(2,1)}) custom-call(bf16[8,64,512]{2,1,0:T(8,128)(2,1)S(1)} %get-tuple-element.11.one, bf16[8,64,128]{2,1,0:T(8,128)(2,1)S(1)} %get-tuple-element.12.two, bf16[4,4,16,768]{3,2,1,0:T(8,128)(2,1)S(1)} %get-tuple-element.13.cols_three, ...), custom_call_target="tpu_custom_call" | custom-call | tf_op jit(solution)/shard_map/pallas_call | solution.py:436

commit v2 on v1

--- a/solution.py
+++ b/solution.py
@@ -34,7 +34,7 @@
 
 
 def windows_two(own, before, after):
-    return ((own[0], own[2]), (own[1], own[3]), (own[2], after(0)), (before(3), own[1]))
+    return ((before(3), own[1]), (own[0], own[2]), (own[1], own[3]), (own[2], after(0)))
 
 
 def windows_three(own, before, after):
@@ -70,19 +70,20 @@
             fill(put, tiles, dx, dy, near, windows)
 
 
-def convolve(side, planes, cols, band):
-    width = cols.shape[-1]
-    left = jnp.concatenate(
-        [
-            jnp.concatenate(
-                [cols[plane + a, c : c + side].reshape(side * 16, width) for plane in planes], axis=0
-            )
-            for a in range(3)
-            for c in range(3)
-        ],
-        axis=1,
-    )
-    return jnp.dot(left, band, preferred_element_type=F32)
+def columns(side, cols, planes, rows_of_taps, lanes, with_halo):
+    def block(plane, c):
+        if not with_halo and plane in (0, side + 1):
+            return jnp.zeros((side * 16, lanes[0].stop - lanes[0].start), BF16)
+        return [cols[plane, c : c + side, :, at].reshape(side * 16, at.stop - at.start) for at in lanes]
+
+    def rows(a, c):
+        blocks = [block(plane + a, c) for plane in planes]
+        return jnp.concatenate(
+            [part if not isinstance(part, list) else part[t] for t in range(len(lanes)) for part in blocks],
+            axis=0,
+        )
+
+    return jnp.concatenate([rows(a, c) for a in rows_of_taps for c in range(3)], axis=1)
 
 
 def build_band_one(source, band):
@@ -102,23 +103,29 @@
             band[to, 128:256] = right
 
 
-def build_band_two(source, band):
-    @pl.loop(0, 9)
-    def _(pair):
-        minus, same, plus = (source[3 * pair + e] for e in range(3))
-        blank = jnp.zeros_like(same)
-        rows = ((same, minus), (plus, same), (blank, plus), (minus, blank))
-        for at, (left, right) in enumerate(rows):
-            to = pl.ds(pl.multiple_of(512 * pair + 128 * at, 128), 128)
-            band[to, 0:128] = left
-            band[to, 128:256] = right
-
-
-def fused(nb, feat, occ, conv_one, kernel_one, conv_two_hbm, kernel_two_hbm, conv_three_hbm,
-          out_one, out_two, cols_three, pooled_three, conv_three,
+WIDE_ONE = (slice(0, 384),)
+WIDE_TWO = (slice(0, 384), slice(128, 512))
+WIDE_THREE = (slice(0, 768),)
+
+
+def dot(left, right):
+    return jnp.dot(left, right, preferred_element_type=F32)
+
+
+def halo_sums(side, cols, lanes, weights):
+    for plane, a in ((0, 0), (side - 1, 2)):
+        left = columns(side, cols, (plane,), (a,), lanes, True)
+        depth = left.shape[1]
+        yield plane, dot(left, weights(a, depth))
+
+
+def fused(nb_hbm, feat_hbm, occ_hbm, conv_one_hbm, kernel_one_hbm,
+          conv_two_hbm, kernel_two_hbm, conv_three_hbm,
+          out_one, out_two, cols_three, pooled_three, early_three, conv_three,
+          nb, feat, occ, conv_one, kernel_one, conv_two, kernel_two,
           field_one, field_two, field_three, cols_one, cols_two, done_one, done_two,
-          band_one, band_two, conv_two, kernel_two, near, words, tests, pooled_two, wide,
-          outgoing, incoming, load_sems, send_sems, recv_sems):
+          band_one, early_one, early_two, near, words, tests, pooled_two, wide,
+          choose, spread, regroup, outgoing, incoming, load_sems, send_sems, recv_sems):
     me = lax.axis_index("morton")
     count = lax.axis_size("morton")
     has_low, has_high = me > 0, me < count - 1
@@ -128,7 +135,11 @@
     loads = [
         pltpu.make_async_copy(source, target, load_sems.at[at])
         for at, (source, target) in enumerate(
-            ((conv_two_hbm, conv_two), (kernel_two_hbm, kernel_two), (conv_three_hbm, conv_three))
+            (
+                (nb_hbm, nb), (occ_hbm, occ), (feat_hbm, feat), (conv_one_hbm, conv_one),
+                (kernel_one_hbm, kernel_one), (conv_two_hbm, conv_two),
+                (kernel_two_hbm, kernel_two), (conv_three_hbm, conv_three),
+            )
         )
     ]
     for load in loads:
@@ -180,13 +191,20 @@
             for level in range(3):
                 incoming[level, source] = jnp.zeros(incoming.shape[2:], BF16)
 
+    row, lane = iota((256, 256), 0), iota((256, 256), 1)
+    spread[...] = (lane == 2 * (row % 128) + row // 128).astype(F32).astype(BF16)
+    regroup[...] = ((lane // 8 == row % 32) & (lane % 8 == row // 32)).astype(F32).astype(BF16)
+    choose[...] = (iota((128, 256), 1) // 2 == iota((128, 256), 0)).astype(F32).astype(BF16)
+    upper = (iota((BRICKS, 128), 1) >= 64).astype(I32)
+    for at in range(16):
+        tests[at] = jnp.left_shift(jnp.ones((BRICKS, 128), I32), 2 * at + upper)
+
+    loads[0].wait()
+    loads[1].wait()
     for tap in range(27):
         near[tap] = jnp.broadcast_to(nb[:, tap : tap + 1], (BRICKS, 128))
     for word in range(16):
         words[word] = jnp.broadcast_to(occ[:, word : word + 1], (BRICKS, 128))
-    upper = (iota((BRICKS, 128), 1) >= 64).astype(I32)
-    for at in range(16):
-        tests[at] = jnp.left_shift(jnp.ones((BRICKS, 128), I32), 2 * at + upper)
     for i in range(4):
         for part in range(2):
             word = words[4 * i + part] | words[4 * i + 2 + part]
@@ -203,7 +221,7 @@
         bit = words[2 * i + j // 4] & tests[4 * (j % 4) + q]
         return jnp.where(bit != 0, value, 0.0)
 
-    choose = (iota((128, 256), 1) // 2 == iota((128, 256), 0)).astype(F32).astype(BF16)
+    loads[2].wait()
     odd = iota((64, 256), 1) % 2 == 1
     for half in range(2):
         lanes = slice(256 * half, 256 * half + 256)
@@ -214,7 +232,7 @@
                 zero = jnp.zeros_like(value)
                 rows += [jnp.where(odd, zero, value), jnp.where(odd, value, zero)]
             both = lax.dot_general(
-                choose, jnp.concatenate(rows, axis=0), (((1,), (1,)), ((), ())),
+                choose[...], jnp.concatenate(rows, axis=0), (((1,), (1,)), ((), ())),
                 preferred_element_type=F32,
             )
             for step in range(2):
@@ -239,31 +257,27 @@
 
     pl.semaphore_wait(barrier, jnp.minimum(me, 1) + jnp.minimum(count - 1 - me, 1))
     send(0)
+    loads[3].wait()
     build_band_one(conv_one, band_one)
 
     @pl.loop(1, 7)
     def _(i):
         fill_plane(8, cols_one, i + 1, own_one(i), 1, near, windows_one)
 
-    loads[0].wait()
-    build_band_two(conv_two, band_two)
-    receive(0, cols_one, windows_one)
-
-    def first_level(planes):
-        sums = convolve(8, planes, cols_one, band_one[...])
-        for p, i in enumerate(planes):
-            for j in range(8):
-                at = 128 * p + 16 * j
-                for t in range(2):
-                    lanes = slice(128 * t, 128 * t + 128)
-                    tiles = []
-                    for h in range(2):
-                        q = 2 * h + t
-                        value = keep_one(i, j, q, jnp.maximum(sums[at + 8 * h : at + 8 * h + 8, lanes], 0.0))
-                        field_one[tile_at(i, j, q), :] = value
-                        tiles.append(value)
-                    done_one[i, j, :, lanes] = pack(*tiles)
-        pooled = [planes[0] // 2, planes[2] // 2]
+    def finish_one(i, sums):
+        for j in range(8):
+            for t in range(2):
+                lanes = slice(128 * t, 128 * t + 128)
+                tiles = []
+                for h in range(2):
+                    q = 2 * h + t
+                    at = 16 * j + 8 * h
+                    value = keep_one(i, j, q, jnp.maximum(sums[at : at + 8, lanes], 0.0))
+                    field_one[tile_at(i, j, q), :] = value
+                    tiles.append(value)
+                done_one[i, j, :, lanes] = pack(*tiles)
+
+    def reduce_one(pooled):
         left = jnp.concatenate(
             [
                 jnp.concatenate(
@@ -280,7 +294,7 @@
             ],
             axis=1,
         )
-        sums = jnp.dot(left, kernel_one[...], preferred_element_type=F32)
+        sums = dot(left, kernel_one[...])
         for p, i in enumerate(pooled):
             for j in range(4):
                 for t in range(2):
@@ -290,33 +304,67 @@
                         keep = (pooled_two[i, j] & (3 << (2 * q))) != 0
                         field_two[i, j, q] = jnp.where(keep, jnp.maximum(sums[at : at + 8], 0.0), 0.0)
 
-    first_level((0, 1, 6, 7))
+    def own_two(i):
+        return lambda j: [field_two[i, j, q] for q in range(4)]
+
+    sums = dot(columns(8, cols_one, range(8), range(3), WIDE_ONE, False), band_one[...])
+    for i in range(8):
+        part = sums[128 * i : 128 * i + 128]
+        if i in (0, 7):
+            early_one[i // 7] = part
+        else:
+            finish_one(i, part)
+    loads[4].wait()
+    reduce_one((1, 2))
+    receive(0, cols_one, windows_one)
+    for i, sums in halo_sums(8, cols_one, WIDE_ONE, lambda a, depth: band_one[a * depth : (a + 1) * depth]):
+        finish_one(i, early_one[i // 7] + sums)
+    reduce_one((0, 3))
     for to, i in enumerate((0, 3)):
         for j in range(4):
-            stage(1, to, j, [field_two[i, j, q] for q in range(4)])
+            stage(1, to, j, own_two(i)(j))
     send(1)
-    first_level((2, 3, 4, 5))
-
-    for i in range(4):
-        fill_plane(4, cols_two, i + 1, lambda j, i=i: [field_two[i, j, q] for q in range(4)],
-                   1, near, windows_two)
-    receive(1, cols_two, windows_two)
-
-    sums = convolve(4, range(4), cols_two, band_two[...])
-    for i in range(4):
+
+    def finish_two(i, sums):
         for j in range(4):
-            at = 64 * i + 16 * j
             for t in range(2):
-                lanes = slice(128 * t, 128 * t + 128)
                 tiles = []
                 for h in range(2):
                     q = 2 * h + t
+                    at = 64 * t + 16 * j + 8 * h
                     keep = (pooled_two[i, j] & (3 << (2 * q))) != 0
-                    value = jnp.where(keep, jnp.maximum(sums[at + 8 * h : at + 8 * h + 8, lanes], 0.0), 0.0)
-                    wide[pl.ds(16 * i + 4 * j + q, 8, stride=64), :] = value
-                    tiles.append(value)
-                done_two[i, j, :, lanes] = pack(*tiles)
-    loads[1].wait()
+                    tiles.append(jnp.where(keep, jnp.maximum(sums[at : at + 8], 0.0), 0.0))
+                done_two[i, j, :, 128 * t : 128 * t + 128] = pack(*tiles)
+
+    for i in range(4):
+        fill_plane(4, cols_two, i + 1, own_two(i), 1, near, windows_two)
+    loads[5].wait()
+    sums = dot(
+        columns(4, cols_two, range(4), range(3), WIDE_TWO, False),
+        conv_two[...].reshape(27 * 128, 128),
+    )
+    for i in range(4):
+        part = jnp.concatenate([sums[256 * t + 64 * i : 256 * t + 64 * i + 64] for t in range(2)], axis=0)
+        if i in (0, 3):
+            early_two[i // 3] = part
+        else:
+            finish_two(i, part)
+
+    for half in range(2):
+        left = []
+        for b in range(BRICKS):
+            turned = field_one[pl.ds(1024 * half + b, 128, stride=8), :].astype(BF16).T
+            left.append(jnp.concatenate([turned[0:64], turned[64:128]], axis=1))
+        sums = dot(jnp.concatenate(left, axis=0), spread[...])
+        for b in range(BRICKS):
+            out_one[b, :, 256 * half : 256 * half + 256] = sums[64 * b : 64 * b + 64].astype(BF16)
+
+    receive(1, cols_two, windows_two)
+    for i, sums in halo_sums(
+        4, cols_two, WIDE_TWO, lambda a, depth: conv_two[9 * a : 9 * a + 9].reshape(depth, 128)
+    ):
+        finish_two(i, early_two[i // 3] + sums)
+    loads[6].wait()
     left = jnp.concatenate(
         [
             jnp.concatenate(
@@ -327,7 +375,7 @@
         ],
         axis=1,
     )
-    sums = jnp.dot(left, kernel_two[...], preferred_element_type=F32)
+    sums = dot(left, kernel_two[...])
     for i in range(2):
         for j in range(2):
             at = 32 * i + 16 * j
@@ -344,23 +392,18 @@
     for i in range(2):
         fill_plane(2, cols_three, i + 1, lambda j, i=i: [field_three[i, j, q] for q in range(4)],
                    1, near, windows_three)
+    loads[7].wait()
+    early_three[...] = dot(
+        columns(2, cols_three, range(2), range(3), WIDE_THREE, False),
+        conv_three[...].reshape(27 * 256, 256),
+    )
+    turned = dot(regroup[...], done_two[...].reshape(256, 256))
+    for t in range(2):
+        wide[pl.ds(t, 256, stride=2), :] = turned[:, 128 * t : 128 * t + 128]
     out_two[...] = wide[...].reshape(BRICKS, 64, 128).astype(BF16)
 
-    spread = (
-        iota((256, 256), 1) == 2 * (iota((256, 256), 0) % 128) + iota((256, 256), 0) // 128
-    ).astype(F32).astype(BF16)
-    for half in range(2):
-        left = []
-        for b in range(BRICKS):
-            turned = field_one[pl.ds(1024 * half + b, 128, stride=8), :].T
-            left.append(jnp.concatenate([turned[0:64], turned[64:128]], axis=1).astype(BF16))
-        sums = jnp.dot(jnp.concatenate(left, axis=0), spread, preferred_element_type=F32)
-        for b in range(BRICKS):
-            out_one[b, :, 256 * half : 256 * half + 256] = sums[64 * b : 64 * b + 64].astype(BF16)
-
     receive(2, cols_three, windows_three)
 
-    loads[2].wait()
     for level in range(3):
         for to in range(2):
             @pl.when(sides[to][0])
@@ -368,7 +411,7 @@
                 transfer(level, to).wait_send()
 
 
-def last_level(one, two, cols_three, pooled_three, conv_three,
+def last_level(one, two, cols_three, pooled_three, early_three, conv_three,
                out_one, out_two, out_three, wide, sems):
     copies = [
         pltpu.make_async_copy(one, out_one, sems.at[0]),
@@ -376,10 +419,12 @@
     ]
     for copy in copies:
         copy.start()
-    sums = convolve(2, range(2), cols_three, conv_three[...].reshape(27 * 256, 256))
-    for i in range(2):
+    for i, sums in halo_sums(
+        2, cols_three, WIDE_THREE, lambda a, depth: conv_three[9 * a : 9 * a + 9].reshape(depth, 256)
+    ):
+        sums = early_three[32 * i : 32 * i + 32] + sums
         for j in range(2):
-            at = 32 * i + 16 * j
+            at = 16 * j
             for h in range(2):
                 keep = (pooled_three[i, j] & (15 << (4 * h))) != 0
                 for t in range(2):
@@ -398,49 +443,52 @@
     vm = pl.BlockSpec(memory_space=pltpu.VMEM)
     hbm = pl.BlockSpec(memory_space=pltpu.HBM)
     kernel_two = second_reduce_kernel.reshape(1024, 256)
+    features, first_kernel = jnp.swapaxes(features, 1, 2), first_reduce_kernel.reshape(512, 128)
     scratch = [
+        (neighbours.shape, I32), (features.shape, BF16), (occupancy.shape, I32),
+        (conv_one.shape, BF16), (first_kernel.shape, BF16), (conv_two.shape, BF16), (kernel_two.shape, BF16),
         ((2048, 128), F32), ((4, 4, 4, BRICKS, 128), F32), ((2, 2, 4, BRICKS, 128), F32),
         ((10, 10, 16, 384), BF16), ((6, 6, 16, 512), BF16),
         ((8, 8, 16, 256), BF16), ((4, 4, 16, 256), BF16),
-        ((9 * 384, 256), BF16), ((9 * 512, 256), BF16),
-        (conv_two.shape, BF16), (kernel_two.shape, BF16),
+        ((9 * 384, 256), BF16), ((2, 128, 256), F32), ((2, 128, 128), F32),
         ((27, BRICKS, 128), I32), ((16, BRICKS, 128), I32), ((16, BRICKS, 128), I32),
         ((4, 4, BRICKS, 128), I32), ((512, 128), F32),
+        ((128, 256), BF16), ((256, 256), BF16), ((256, 256), BF16),
         ((3, 2, 8, 16, 256), BF16), ((3, 2, 8, 16, 256), BF16),
     ]
     shapes = [
         jax.ShapeDtypeStruct((BRICKS, 64, 512), BF16),
         jax.ShapeDtypeStruct((BRICKS, 64, 128), BF16),
     ]
-    first, second, cols, pooled, weights = pl.pallas_call(
+    first, second, cols, pooled, early, weights = pl.pallas_call(
         fused,
         out_shape=shapes
         + [
             jax.ShapeDtypeStruct((4, 4, 16, 768), BF16),
             jax.ShapeDtypeStruct((2, 2, BRICKS, 128), I32),
+            jax.ShapeDtypeStruct((64, 256), F32),
             jax.ShapeDtypeStruct(conv_three.shape, BF16),
         ],
-        in_specs=[vm, vm, vm, vm, vm, hbm, hbm, hbm],
-        out_specs=[vm] * 5,
+        in_specs=[hbm] * 8,
+        out_specs=[vm] * 6,
         scratch_shapes=[pltpu.VMEM(shape, dtype) for shape, dtype in scratch]
-        + [pltpu.SemaphoreType.DMA((3,)), pltpu.SemaphoreType.DMA((3, 2)),
+        + [pltpu.SemaphoreType.DMA((8,)), pltpu.SemaphoreType.DMA((3, 2)),
            pltpu.SemaphoreType.DMA((3, 2))],
         compiler_params=pltpu.CompilerParams(
             collective_id=0, has_side_effects=True, vmem_limit_bytes=36 << 20
         ),
     )(*(
         pltpu.with_memory_space_constraint(x, pltpu.HBM)
-        for x in (neighbours, jnp.swapaxes(features, 1, 2), occupancy, conv_one,
-                  first_reduce_kernel.reshape(512, 128), conv_two, kernel_two, conv_three)
+        for x in (neighbours, features, occupancy, conv_one, first_kernel, conv_two, kernel_two, conv_three)
     ))
     first, second, third = pl.pallas_call(
         last_level,
         out_shape=shapes + [jax.ShapeDtypeStruct((BRICKS, 8, 256), BF16)],
-        in_specs=[vm] * 5,
+        in_specs=[vm] * 6,
         out_specs=[hbm, hbm, vm],
         scratch_shapes=[pltpu.VMEM((2, 64, 128), F32), pltpu.SemaphoreType.DMA((2,))],
         compiler_params=pltpu.CompilerParams(vmem_limit_bytes=16 << 20),
-    )(first, second, cols, pooled, weights)
+    )(first, second, cols, pooled, early, weights)
     return jnp.swapaxes(first, 1, 2), second, third
 
 

time: 18.1 us -> 17.3 us (0.956)
  the two profiles are of different devices: /device:TPU:7 before, /device:TPU:1 now
where the time goes in v2:
time: 17.3 us; the launch traced here: 17.1 us
  Pallas kernels  16.5 us (95%)
  between operations  0.64 us (4%)
    pallas_call x1, Pallas kernels, on_device(): pl.pallas_call(fused, out_shape=shapes + [jax.ShapeDtypeStruct((4, 4, 16,...  14.7 us
    pallas_call x1, Pallas kernels, on_device(): pl.pallas_call(last_level, out_shape=shapes + [jax.ShapeDtypeStruct((BRIC...  1.75 us

profile of v2, /device:TPU:1, one launch (start us, length us, event | category | flops | bytes accessed | tf_op | source)
XLA Modules:
  0.0 17.1 jit_solution(18327034481749596519)
XLA Ops:
  0.6 14.7 %shard_map.103 = (bf16[8,64,512]{2,1,0:T(8,128)(2,1)S(1)}, bf16[8,64,128]{2,1,0:T(8,128)(2,1)S(1)}, bf16[4,4,16,768]{3,2,1,0:T(8,128)(2,1)S(1)}, s32[2,2,8,128]{...) custom-call(s32[8,27]{1,0:T(8,128)} %nb_hbm.1, bf16[8,64,512]{2,1,0:T(8,128)(2,1)} %bitcast.4, ...), custom_call_target="tpu_custom_call" | custom-call | tf_op jit(solution)/shard_map/pallas_call | solution.py:463
  15.4 1.8 %shard_map.104 = (bf16[8,64,512]{2,1,0:T(8,128)(2,1)}, bf16[8,64,128]{2,1,0:T(8,128)(2,1)}, bf16[8,8,256]{2,1,0:T(8,128)(2,1)}) custom-call(bf16[8,64,512]{2,1,0:T(8,128)(2,1)S(1)} %get-tuple-element.12.one, bf16[8,64,128]{2,1,0:T(8,128)(2,1)S(1)} %get-tuple-element.13.two, bf16[4,4,16,768]{3,2,1,0:T(8,128)(2,1)S(1)} %get-tuple-element.14.cols_three, ...), custom_call_target="tpu_custom_call" | custom-call | tf_op jit(solution)/shard_map/pallas_call | solution.py:484
